TPU v7x, 32 devices: a whole 2x2x4 slice. The times are simulated.
32 devices in a mesh: src: 4 (over z), dst: 8 (over y, x, core).
Axes of the slice: x: 2, y: 2, z: 4, core: 2. Of those that a mesh axis runs over, the one named last changes fastest.
Arguments:
- table: float32 [65536, 400], P(('src', 'dst')), may hold values from -2 to 2
- state: float32 [65536], P(('src', 'dst')), may hold values from 0.0001 to 0.01
- relations: float32 [4096, 400], replicated, may hold values from -4 to 4
- rel_ids: int32 [65536], P(('src', 'dst')), may hold values from 0 to 4095
- block_list: int32 [32, 32], P(('src', 'dst')), may hold values from 0 to 15
- src_pos: int32 [65536], P(('src', 'dst')), may hold values from 0 to 4095, as said below
- dst_pos: int32 [65536], P(('src', 'dst')), may hold values from 0 to 4095, as said below
- neg_pos: int32 [4096], P(('src', 'dst')), may hold values from 0 to 4095, as said below
Outputs:
- new_table: float32 [65536, 400], P(('src', 'dst'))
- new_state: float32 [65536], P(('src', 'dst'))
Inputs may be any that keep to these rules, and one draw needn't show every extreme that they name: Each entry is owner * 128 + row of a block the device requested; one device's src_pos, dst_pos and neg_pos name the same 16 owners, and its src_pos names each of them. `dst_pos`: rows of the same 16 owners as the device's src_pos. `neg_pos`: rows of the same 16 owners as the device's src_pos.
All inputs are finite; a program needn't handle non-finite values.
Results may differ from a plain program's by a relative error of at most 0.0004.
The roundings to bfloat16 on the way count: a program that leaves them out, or rounds other values in their place, can miss the bound.
Values may be sent and summed in bfloat16 or wider, within the bound.
No kernel may reach another device: no remote copies, remote signals or barrier semaphores. Data moves between devices by JAX's collectives and lax.ppermute only.
A program may use at most 192 MiB of HBM per device.

v0:
```python
import jax
import jax.numpy as jnp
from jax import lax
from jax.sharding import PartitionSpec as P

BLK = 128


def per_device(table, state, relations, rel_ids, block_list, src_pos, dst_pos, neg_pos):
    devices = lax.axis_size(("src", "dst"))
    rows_dev, width = table.shape
    blocks = rows_dev // BLK
    wanted = lax.all_to_all(
        block_list.reshape(devices, 1), ("src", "dst"), split_axis=0, concat_axis=0, tiled=True
    )
    asked = wanted.reshape(devices)
    outgoing = table.reshape(blocks, BLK, width).astype(jnp.bfloat16)[asked]
    fetched = lax.all_to_all(outgoing, ("src", "dst"), split_axis=0, concat_axis=0, tiled=True)
    flat = fetched.reshape(devices * BLK, width)
    source = flat[src_pos].astype(jnp.float32)
    target = flat[dst_pos].astype(jnp.float32)
    own_negs = flat[neg_pos]
    negs = lax.all_gather(own_negs, "dst", axis=0, tiled=True)
    operator = relations[rel_ids]
    u_full = source * operator
    u_half = u_full.astype(jnp.bfloat16)
    positive = jnp.sum(u_full * target, axis=1)
    scores = jnp.dot(u_half, negs.T, preferred_element_type=jnp.float32)
    g_pos = -jax.nn.sigmoid(-positive)
    g_neg = (jax.nn.sigmoid(scores) / negs.shape[0]).astype(jnp.bfloat16)
    grad_u = g_pos[:, None] * target + jnp.dot(g_neg, negs, preferred_element_type=jnp.float32)
    grad_src = grad_u * operator
    grad_dst = g_pos[:, None] * u_full
    own_neg_grad = lax.psum_scatter(
        jnp.dot(g_neg.T, u_half, preferred_element_type=jnp.float32).astype(jnp.bfloat16),
        "dst",
        scatter_dimension=0,
        tiled=True,
    ).astype(jnp.float32)
    slots = jnp.zeros((devices * BLK, width), jnp.float32)
    slots = slots.at[src_pos].add(grad_src).at[dst_pos].add(grad_dst).at[neg_pos].add(own_neg_grad)
    returned = lax.all_to_all(
        slots.reshape(devices, BLK, width), ("src", "dst"), split_axis=0, concat_axis=0, tiled=True
    )
    selector = (asked[None, :] == jnp.arange(blocks, dtype=jnp.int32)[:, None]).astype(jnp.float32)
    grad = jnp.einsum("bq,qrw->brw", selector, returned, precision=lax.Precision.HIGHEST).reshape(
        rows_dev, width
    )
    new_state = state + jnp.mean(grad * grad, axis=1)
    new_table = table - 0.1 * grad / (jnp.sqrt(new_state)[:, None] + 1e-10)
    return (new_table, new_state)


def solution(mesh):
    in_specs = (
        P(("src", "dst"), None),
        P(("src", "dst")),
        P(),
        P(("src", "dst")),
        P(("src", "dst"), None),
        P(("src", "dst")),
        P(("src", "dst")),
        P(("src", "dst")),
    )
    out_specs = (P(("src", "dst"), None), P(("src", "dst")))
    return jax.shard_map(
        per_device, mesh=mesh, in_specs=in_specs, out_specs=out_specs, check_vma=False
    )
```

profile of v0, /device:TPU:0, one launch (start us, length us, event | category | flops | bytes accessed | tf_op | source)
XLA Modules:
  0.0 411.0 jit_solution(8003938198328237329)
XLA Ops:
  8.5 7.3 %all-to-all-start = ((s32[32,1,1]{2,1,0:T(1,128)}), s32[32,1,1]{2,1,0:T(1,128)S(1)}, u32[]{:S(2)}, u32[]{:S(2)}) async-start(s32[32,1,1]{2,1,0:T(1,128)} %copy.54), calls=%async_computation | async-start | bytes 32768 | tf_op jit(solution)/shard_map/all_to_all | solution.py:13
  15.8 2.1 copy_bitcast_fusion
  18.0 4.9 %all-to-all-done = s32[32,1,1]{2,1,0:T(1,128)S(1)} async-done(((s32[32,1,1]{2,1,0:T(1,128)}), s32[32,1,1]{2,1,0:T(1,128)S(1)}, u32[]{:S(2)}, u32[]{:S(2)}) %all-to-all-start) | async-done | bytes 160 | tf_op jit(solution)/shard_map/all_to_all | solution.py:13
  23.6 2.7 gather_fusion
  26.2 3.5 all-to-all-start.1
  29.8 8.5 %copy.59 = f32[4096,400]{1,0:T(8,128)} copy(f32[4096,400]{0,1:T(8,128)} %param.10) | data formatting | bytes 13107200 | tf_op args[2]
  38.4 12.9 %gather_fusion.2 = f32[2048,400]{1,0:T(8,128)} fusion(f32[4096,400]{1,0:T(8,128)} %copy.59, s32[2048]{0:T(1024)S(1)} %fusion.9), kind=kCustom, calls=%fused_computation.2 | custom fusion | bytes 6561792 | tf_op jit(solution)/shard_map/gather | solution.py:24
  51.3 3.8 copy.60
  55.2 48.9 %all-to-all-done.1 = bf16[32,128,400]{1,2,0:T(8,128)(2,1)} async-done(((bf16[32,128,400]{1,2,0:T(8,128)(2,1)}), bf16[32,128,400]{1,2,0:T(8,128)(2,1)}, u32[]{:S(2)}, u32[]{:S(2)}) %all-to-all-start.1) | async-done | bytes 3276832 | tf_op jit(solution)/shard_map/all_to_all | solution.py:18
  104.1 6.0 %copy.72 = bf16[32,128,400]{2,1,0:T(8,128)(2,1)} copy(bf16[32,128,400]{1,2,0:T(8,128)(2,1)} %all-to-all-done.1) | data formatting | bytes 6553600 | tf_op jit(solution)/shard_map/reshape | solution.py:19
  110.1 3.6 gather_fusion.4
  113.7 11.9 %all-gather = bf16[1024,400]{1,0:T(8,128)(2,1)} all-gather(bf16[128,400]{1,0:T(8,128)(2,1)S(1)} %gather_fusion.4), channel_id=2, replica_groups=mesh['src'=4,'dst'=8] {'dst'}, dimensions={0}, use_global_device_ids=true | all-gather | bytes 921600 | tf_op jit(solution)/shard_map/all_gather | solution.py:23
  125.6 12.0 %gather_fusion.3 = bf16[2048,400]{1,0:T(8,128)(2,1)} fusion(bf16[4096,400]{1,0:T(8,128)(2,1)} %bitcast.33, s32[2048]{0:T(1024)S(1)} %get-tuple-element.7), kind=kCustom, calls=%fused_computation.3 | custom fusion | bytes 3284992 | tf_op jit(solution)/shard_map/gather | solution.py:21
  137.6 12.0 %gather_fusion.1 = bf16[2048,400]{1,0:T(8,128)(2,1)} fusion(bf16[4096,400]{1,0:T(8,128)(2,1)} %bitcast.34, s32[2048]{0:T(1024)S(1)} %get-tuple-element.8), kind=kCustom, calls=%fused_computation.1 | custom fusion | bytes 3284992 | tf_op jit(solution)/shard_map/gather | solution.py:20
  149.5 3.9 copy.58
  153.4 3.8 copy.62
  157.3 2.8 fusion.4
  160.0 4.1 %multiply_convert_fusion = bf16[2048,1024]{1,0:T(8,128)(2,1)S(1)} fusion(bf16[1024,400]{1,0:T(8,128)(2,1)S(1)} %copy-done.3, f32[2048,400]{0,1:T(8,128)S(1)} %copy.60, bf16[2048,400]{0,1:T(8,128)(2,1)S(1)} %copy-done), kind=kOutput, calls=%fused_computation.8 | convolution fusion | flops 1690664960 | bytes 9928704 | tf_op jit(solution)/shard_map/dot_general | solution.py:28
  164.2 1.9 copy-done.1
  166.1 2.9 convolution_convert_fusion
  169.0 2.2 copy.70
  171.2 3.6 broadcast_multiply_fusion.1
  174.8 5.1 %copy.66 = f32[2048,400]{1,0:T(8,128)} copy(f32[2048,400]{0,1:T(8,128)} %broadcast_multiply_fusion.1) | data formatting | bytes 6553600 | tf_op jit(solution)/shard_map/mul | solution.py:33
  179.9 7.0 %fusion.6 = f32[2048,400]{0,1:T(8,128)} fusion(f32[2048,400]{0,1:T(8,128)S(1)} %copy.60, bf16[2048,400]{0,1:T(8,128)(2,1)} %copy.62, bf16[2048,1024]{1,0:T(8,128)(2,1)} %copy-done.1, bf16[1024,400]{1,0:T(8,128)(2,1)} %all-gather, f32[2048]{0:T(1024)S(1)} %divide_negate_fusion), kind=kOutput, calls=%fused_computation.17 | convolution fusion | flops 1680998400 | bytes 13213696 | tf_op jit(solution)/shard_map/dot_general | solution.py:31
  186.9 5.0 %copy.65 = f32[2048,400]{1,0:T(8,128)} copy(f32[2048,400]{0,1:T(8,128)} %fusion.6) | data formatting | bytes 6553600 | tf_op jit(solution)/shard_map/mul | solution.py:32
  191.9 17.2 %scatter_custom_fusion = f32[4096,400]{1,0:T(8,128)} fusion(s32[2048]{0:T(1024)S(1)} %get-tuple-element.9, f32[2048,400]{1,0:T(8,128)} %copy.65, f32[]{:T(128)} %constant.9.clone.1), kind=kCustom, calls=%fused_computation.11 | custom fusion | flops 819200 | bytes 6554112 | tf_op jit(solution)/shard_map/scatter-add | solution.py:41
  209.0 19.8 %scatter_fusion = f32[4096,400]{1,0:T(8,128)} fusion(f32[4096,400]{1,0:T(8,128)} %scatter_custom_fusion, s32[2048]{0:T(1024)S(1)} %get-tuple-element.6, f32[2048,400]{1,0:T(8,128)} %copy.66), kind=kCustom, calls=%fused_computation.6 | custom fusion | flops 819200 | bytes 9838592 | tf_op jit(solution)/shard_map/scatter-add | solution.py:41
  229.9 7.9 %scatter_fusion.1 = f32[4096,400]{1,0:T(8,128)} fusion(f32[4096,400]{1,0:T(8,128)} %scatter_fusion, s32[128]{0:T(128)S(1)} %compare_select_fusion.3, f32[128,400]{1,0:T(8,128)S(1)} %copy.67), kind=kCustom, calls=%fused_computation.7 | custom fusion | flops 51200 | bytes 614912 | tf_op jit(solution)/shard_map/scatter-add | solution.py:41
  237.8 8.7 %copy.68 = f32[32,128,400]{1,2,0:T(8,128)} copy(f32[32,128,400]{2,1,0:T(8,128)} %bitcast.35) | data formatting | bytes 13107200 | tf_op jit(solution)/shard_map/reshape | solution.py:43
  246.5 149.1 %all_to_all.22 = f32[32,128,400]{1,2,0:T(8,128)S(1)} all-to-all(f32[32,128,400]{1,2,0:T(8,128)} %copy.68), channel_id=1, replica_groups=mesh['src'=4,'dst'=8] {'src','dst'}, dimensions={0} | all-to-all | bytes 13107200 | tf_op jit(solution)/shard_map/all_to_all | solution.py:42
  395.6 4.5 %multiply_reduce_fusion = (f32[16,128]{1,0:T(8,128)S(1)}, f32[16,128,400]{1,0,2:T(8,128)S(1)}) fusion(f32[32,128,400]{1,2,0:T(8,128)S(1)} %all_to_all.22, s32[32]{0:T(128)S(1)} %reduce.1), kind=kOutput, calls=%fused_computation.20 | convolution fusion | flops 317028864 | bytes 9838720 | tf_op jit(solution)/shard_map/bq,qrw->brw/dot_general | solution.py:46
  400.7 3.5 fusion.7
  (33 shorter events, 3.9 us)
Async XLA Ops:
  8.5 14.4 %all-to-all-start = ((s32[32,1,1]{2,1,0:T(1,128)}), s32[32,1,1]{2,1,0:T(1,128)S(1)}, u32[]{:S(2)}, u32[]{:S(2)}) async-start(s32[32,1,1]{2,1,0:T(1,128)} %copy.54), calls=%async_computation | async-start | bytes 32768 | tf_op jit(solution)/shard_map/all_to_all | solution.py:13
  26.2 77.8 %all-to-all-start.1 = ((bf16[32,128,400]{1,2,0:T(8,128)(2,1)}), bf16[32,128,400]{1,2,0:T(8,128)(2,1)}, u32[]{:S(2)}, u32[]{:S(2)}) async-start(bf16[32,128,400]{1,2,0:T(8,128)(2,1)} %gather_fusion), calls=%async_computation.1 | async-start | bytes 6553600 | tf_op jit(solution)/shard_map/all_to_all | solution.py:18
  29.8 8.6 %copy-start.6 = (s32[2048]{0:T(1024)S(1)}, s32[2048]{0:T(1024)}, u32[]{:S(2)}) copy-start(s32[2048]{0:T(1024)} %param.11) | copy-start | bytes 24580
  29.8 199.0 %reduce-scatter.4.cloned.1.call-start = ((), (), s32[]{:S(2)}) async-start(), calls=%async_computation.4 | async-start | bytes 1179648
  51.3 3.8 copy-start.8
  51.3 3.8 copy-start.4
  51.3 3.8 copy-start.5
  157.2 2.8 copy-start
  157.2 2.8 copy-start.3
  164.2 1.9 copy-start.1
  395.6 4.5 %copy-start.7 = (f32[2048]{0:T(1024)S(1)}, f32[2048]{0:T(1024)}, u32[]{:S(2)}) copy-start(f32[2048]{0:T(1024)} %param.9) | copy-start | bytes 24580
  395.6 5.1 %copy-start.2 = (f32[2048,400]{0,1:T(8,128)S(1)}, f32[2048,400]{0,1:T(8,128)}, u32[]{:S(2)}) copy-start(f32[2048,400]{0,1:T(8,128)} %param.8) | copy-start | bytes 9830404
Sparse Core Ops, SparseCore 0:
  171.4 34.9 reduce-scatter.3
where the time goes:
time: 412 us; the launch traced here: 411 us
  blocking collectives  161 us (39%)
  local copies, waits for them, and re-layouts  94.6 us (23%)
  other arithmetic  58.1 us (14%)
  waiting for transfers between devices  53.8 us (13%)
  matrix products  18.4 us (4%)
  between operations  14.2 us (3%)
  starting transfers between devices  10.9 us (3%)
    all_to_all x1, blocking collectives, per_device(): lax.all_to_all(slots.reshape(devices, BLK, width), ('src', 'dst'), split_...  149 us
    all_to_all x1, waiting for transfers between devices, per_device(): lax.all_to_all(outgoing, ('src', 'dst'), split_axis=0, concat_axis=0, til...  48.9 us
    scatter-add x3, other arithmetic, per_device(): slots.at[src_pos].add(grad_src).at[dst_pos].add(grad_dst).at[neg_pos]  44.8 us
    gather x2, local copies, waits for them, and re-layouts, per_device(): operator = relations[rel_ids]  16.7 us
    gather x2, local copies, waits for them, and re-layouts, per_device(): source = flat[src_pos].astype(jnp.float32)  15.8 us
    gather x2, local copies, waits for them, and re-layouts, per_device(): target = flat[dst_pos].astype(jnp.float32)  15.8 us
    unnamed x21, local copies, waits for them, and re-layouts  13.7 us
    all_gather x1, blocking collectives, per_device(): negs = lax.all_gather(own_negs, 'dst', axis=0, tiled=True)  11.9 us
  transfers between devices with their start and end apart: 3, of which 2 were waited for; matrix products, arithmetic and copies ran while one was open for 21% of the time, Pallas kernels for 0%

commit v1 on v0

--- a/solution.py
+++ b/solution.py
@@ -20,7 +20,21 @@
     source = flat[src_pos].astype(jnp.float32)
     target = flat[dst_pos].astype(jnp.float32)
     own_negs = flat[neg_pos]
-    negs = lax.all_gather(own_negs, "dst", axis=0, tiled=True)
+    ways, here, step = (lax.axis_size("dst"), lax.axis_index("dst"), own_negs.shape[0])
+    lengths = [n * ways if d == 0 else n for d, n in enumerate(own_negs.shape)]
+    full = lax.dynamic_update_slice_in_dim(
+        jnp.zeros(lengths, own_negs.dtype), own_negs, here * step, axis=0
+    )
+    going_up = going_down = own_negs
+    for far in range(1, ways // 2 + 1):
+        going_up = lax.ppermute(going_up, "dst", [(d, (d + 1) % ways) for d in range(ways)])
+        full = lax.dynamic_update_slice_in_dim(full, going_up, (here - far) % ways * step, axis=0)
+        if 2 * far < ways:
+            going_down = lax.ppermute(going_down, "dst", [(d, (d - 1) % ways) for d in range(ways)])
+            full = lax.dynamic_update_slice_in_dim(
+                full, going_down, (here + far) % ways * step, axis=0
+            )
+    negs = full
     operator = relations[rel_ids]
     u_full = source * operator
     u_half = u_full.astype(jnp.bfloat16)

time: 412 us -> 422 us (1.024)
  blocking collectives: 161 us -> 149 us
  waiting for transfers between devices: 53.8 us -> 64.4 us
  starting transfers between devices: 10.9 us -> 18.9 us
    ppermute x0 -> x7, waiting for transfers between devices: none -> 12 us  [the longest x4 12 us: per_device(): lax.ppermute(going_up, 'dst', [(d, (d + 1) % ways) for d in range(ways)])]
    all_gather x1 -> x0, blocking collectives: 11.9 us -> none  [per_device(): negs = lax.all_gather(own_negs, 'dst', axis=0, tiled=True)]
    ppermute x0 -> x7, starting transfers between devices: none -> 8.02 us  [the longest x3 7.9 us: per_device(): lax.ppermute(going_down, 'dst', [(d, (d - 1) % ways) for d in range(ways)])]
    unnamed x21 -> x29, local copies, waits for them, and re-layouts: 13.7 us -> 13.8 us
  transfers between devices with their start and end apart: 3 -> 10, of which waited for: 2 -> 5; matrix products, arithmetic and copies ran while one was open for 21% -> 29% of each run, Pallas kernels for 0% -> 0%
where the time goes in v1:
time: 422 us; the launch traced here: 420 us
  blocking collectives  149 us (35%)
  local copies, waits for them, and re-layouts  96.5 us (23%)
  waiting for transfers between devices  64.4 us (15%)
  other arithmetic  59 us (14%)
  starting transfers between devices  18.9 us (4%)
  matrix products  18.3 us (4%)
  between operations  14.5 us (3%)
    all_to_all x1, blocking collectives, per_device(): lax.all_to_all(slots.reshape(devices, BLK, width), ('src', 'dst'), split_...  149 us
    all_to_all x1, waiting for transfers between devices, per_device(): lax.all_to_all(outgoing, ('src', 'dst'), split_axis=0, concat_axis=0, til...  47.5 us
    scatter-add x3, other arithmetic, per_device(): slots.at[src_pos].add(grad_src).at[dst_pos].add(grad_dst).at[neg_pos]  44.6 us
    gather x2, local copies, waits for them, and re-layouts, per_device(): operator = relations[rel_ids]  16.7 us
    gather x2, local copies, waits for them, and re-layouts, per_device(): target = flat[dst_pos].astype(jnp.float32)  16.6 us
    gather x2, local copies, waits for them, and re-layouts, per_device(): source = flat[src_pos].astype(jnp.float32)  15.8 us
    unnamed x29, local copies, waits for them, and re-layouts  13.8 us
    ppermute x4, waiting for transfers between devices, per_device(): lax.ppermute(going_up, 'dst', [(d, (d + 1) % ways) for d in range(ways)])  12 us
  transfers between devices with their start and end apart: 10, of which 5 were waited for; matrix products, arithmetic and copies ran while one was open for 29% of the time, Pallas kernels for 0%

profile of v1, /device:TPU:0, one launch (start us, length us, event | category | flops | bytes accessed | tf_op | source)
XLA Modules:
  0.0 420.2 jit_solution(3993552249931156064)
XLA Ops:
  8.5 7.3 %all-to-all-start = ((s32[32,1,1]{2,1,0:T(1,128)}), s32[32,1,1]{2,1,0:T(1,128)S(1)}, u32[]{:S(2)}, u32[]{:S(2)}) async-start(s32[32,1,1]{2,1,0:T(1,128)} %copy.54), calls=%async_computation | async-start | bytes 32768 | tf_op jit(solution)/shard_map/all_to_all | solution.py:13
  18.0 4.9 %all-to-all-done = s32[32,1,1]{2,1,0:T(1,128)S(1)} async-done(((s32[32,1,1]{2,1,0:T(1,128)}), s32[32,1,1]{2,1,0:T(1,128)S(1)}, u32[]{:S(2)}, u32[]{:S(2)}) %all-to-all-start) | async-done | bytes 160 | tf_op jit(solution)/shard_map/all_to_all | solution.py:13
  23.6 2.7 gather_fusion
  26.3 3.5 all-to-all-start.1
  30.0 8.5 %copy.59 = f32[4096,400]{1,0:T(8,128)} copy(f32[4096,400]{0,1:T(8,128)} %param.10) | data formatting | bytes 13107200 | tf_op args[2]
  38.5 13.0 %gather_fusion.2 = f32[2048,400]{1,0:T(8,128)} fusion(f32[4096,400]{1,0:T(8,128)} %copy.59, s32[2048]{0:T(1024)S(1)} %fusion.9), kind=kCustom, calls=%fused_computation.2 | custom fusion | bytes 6561792 | tf_op jit(solution)/shard_map/gather | solution.py:38
  51.5 3.8 copy.60
  56.6 47.5 %all-to-all-done.1 = bf16[32,128,400]{1,2,0:T(8,128)(2,1)} async-done(((bf16[32,128,400]{1,2,0:T(8,128)(2,1)}), bf16[32,128,400]{1,2,0:T(8,128)(2,1)}, u32[]{:S(2)}, u32[]{:S(2)}) %all-to-all-start.1) | async-done | bytes 3276832 | tf_op jit(solution)/shard_map/all_to_all | solution.py:18
  104.1 6.0 %copy.72 = bf16[32,128,400]{2,1,0:T(8,128)(2,1)} copy(bf16[32,128,400]{1,2,0:T(8,128)(2,1)} %all-to-all-done.1) | data formatting | bytes 6553600 | tf_op jit(solution)/shard_map/reshape | solution.py:19
  110.1 3.6 gather_fusion.4
  116.4 12.7 %gather_fusion.3 = bf16[2048,400]{1,0:T(8,128)(2,1)} fusion(bf16[4096,400]{1,0:T(8,128)(2,1)} %bitcast.33, s32[2048]{0:T(1024)} %get-tuple-element.7), kind=kCustom, calls=%fused_computation.3 | custom fusion | bytes 3284992 | tf_op jit(solution)/shard_map/gather | solution.py:21
  129.1 12.0 %gather_fusion.1 = bf16[2048,400]{1,0:T(8,128)(2,1)} fusion(bf16[4096,400]{1,0:T(8,128)(2,1)} %bitcast.34, s32[2048]{0:T(1024)S(1)} %get-tuple-element.8), kind=kCustom, calls=%fused_computation.1 | custom fusion | bytes 3284992 | tf_op jit(solution)/shard_map/gather | solution.py:20
  141.1 3.8 copy.58
  144.9 3.9 copy.62
  148.8 2.7 fusion.4
  155.3 3.0 collective-permute-done.2
  158.3 2.6 collective-permute-start.5
  161.0 3.7 collective-permute-done.4
  164.8 5.2 %collective-permute-done.6 = bf16[128,400]{1,0:T(8,128)(2,1)S(1)} collective-permute-done((bf16[128,400]{1,0:T(8,128)(2,1)S(1)}, bf16[128,400]{1,0:T(8,128)(2,1)S(1)}, u32[]{:S(2)}, u32[]{:S(2)}) %collective-permute-start.6) | collective-permute-done | bytes 102432 | tf_op jit(solution)/shard_map/ppermute | solution.py:30
  170.0 4.1 multiply_convert_fusion
  176.1 2.9 convolution_convert_fusion
  181.2 3.6 broadcast_multiply_fusion.1
  184.8 5.1 %copy.66 = f32[2048,400]{1,0:T(8,128)} copy(f32[2048,400]{0,1:T(8,128)} %broadcast_multiply_fusion.1) | data formatting | bytes 6553600 | tf_op jit(solution)/shard_map/mul | solution.py:47
  189.9 6.9 %fusion.6 = f32[2048,400]{0,1:T(8,128)} fusion(f32[2048,400]{0,1:T(8,128)S(1)} %copy.60, bf16[2048,400]{0,1:T(8,128)(2,1)} %copy.62, bf16[2048,1024]{1,0:T(8,128)(2,1)} %copy-done.1, bf16[1024,400]{1,0:T(8,128)(2,1)} %copy-done.3, f32[2048]{0:T(1024)S(1)} %divide_negate_fusion), kind=kOutput, calls=%fused_computation.17 | convolution fusion | flops 1680998400 | bytes 13213696 | tf_op jit(solution)/shard_map/dot_general | solution.py:45
  196.8 5.0 %copy.65 = f32[2048,400]{1,0:T(8,128)} copy(f32[2048,400]{0,1:T(8,128)} %fusion.6) | data formatting | bytes 6553600 | tf_op jit(solution)/shard_map/mul | solution.py:46
  201.8 16.9 %scatter_custom_fusion = f32[4096,400]{1,0:T(8,128)} fusion(s32[2048]{0:T(1024)} %get-tuple-element.9, f32[2048,400]{1,0:T(8,128)} %copy.65, f32[]{:T(128)} %constant.65.clone.1), kind=kCustom, calls=%fused_computation.11 | custom fusion | flops 819200 | bytes 6554112 | tf_op jit(solution)/shard_map/scatter-add | solution.py:55
  218.7 19.8 %scatter_fusion = f32[4096,400]{1,0:T(8,128)} fusion(f32[4096,400]{1,0:T(8,128)} %scatter_custom_fusion, s32[2048]{0:T(1024)S(1)} %get-tuple-element.6, f32[2048,400]{1,0:T(8,128)} %copy.66), kind=kCustom, calls=%fused_computation.6 | custom fusion | flops 819200 | bytes 9838592 | tf_op jit(solution)/shard_map/scatter-add | solution.py:55
  239.7 7.9 %scatter_fusion.1 = f32[4096,400]{1,0:T(8,128)} fusion(f32[4096,400]{1,0:T(8,128)} %scatter_fusion, s32[128]{0:T(128)S(1)} %copy-done.11, f32[128,400]{1,0:T(8,128)S(1)} %copy.67), kind=kCustom, calls=%fused_computation.7 | custom fusion | flops 51200 | bytes 614912 | tf_op jit(solution)/shard_map/scatter-add | solution.py:55
  247.5 8.7 %copy.68 = f32[32,128,400]{1,2,0:T(8,128)} copy(f32[32,128,400]{2,1,0:T(8,128)} %bitcast.35) | data formatting | bytes 13107200 | tf_op jit(solution)/shard_map/reshape | solution.py:57
  256.2 148.5 %all_to_all.22 = f32[32,128,400]{1,2,0:T(8,128)S(1)} all-to-all(f32[32,128,400]{1,2,0:T(8,128)} %copy.68), channel_id=1, replica_groups=mesh['src'=4,'dst'=8] {'src','dst'}, dimensions={0} | all-to-all | bytes 13107200 | tf_op jit(solution)/shard_map/all_to_all | solution.py:56
  404.8 4.5 %multiply_reduce_fusion = (f32[16,128]{1,0:T(8,128)S(1)}, f32[16,128,400]{1,0,2:T(8,128)S(1)}) fusion(f32[32,128,400]{1,2,0:T(8,128)S(1)} %all_to_all.22, s32[32]{0:T(128)S(1)} %copy-done.9), kind=kOutput, calls=%fused_computation.20 | convolution fusion | flops 317028864 | bytes 9838720 | tf_op jit(solution)/shard_map/bq,qrw->brw/dot_general | solution.py:60
  409.9 3.5 fusion.7
  (63 shorter events, 17.9 us)
Async XLA Ops:
  8.5 14.4 %all-to-all-start = ((s32[32,1,1]{2,1,0:T(1,128)}), s32[32,1,1]{2,1,0:T(1,128)S(1)}, u32[]{:S(2)}, u32[]{:S(2)}) async-start(s32[32,1,1]{2,1,0:T(1,128)} %copy.54), calls=%async_computation | async-start | bytes 32768 | tf_op jit(solution)/shard_map/all_to_all | solution.py:13
  23.5 2.7 copy-start.8
  26.3 77.8 %all-to-all-start.1 = ((bf16[32,128,400]{1,2,0:T(8,128)(2,1)}), bf16[32,128,400]{1,2,0:T(8,128)(2,1)}, u32[]{:S(2)}, u32[]{:S(2)}) async-start(bf16[32,128,400]{1,2,0:T(8,128)(2,1)} %gather_fusion), calls=%async_computation.1 | async-start | bytes 6553600 | tf_op jit(solution)/shard_map/all_to_all | solution.py:18
  29.8 208.7 %reduce-scatter.4.cloned.1.call-start = ((), (), s32[]{:S(2)}) async-start(), calls=%async_computation.4 | async-start | bytes 1179648
  30.0 8.6 %copy-start.6 = (s32[2048]{0:T(1024)S(1)}, s32[2048]{0:T(1024)}, u32[]{:S(2)}) copy-start(s32[2048]{0:T(1024)} %param.11) | copy-start | bytes 24580
  51.5 3.8 copy-start.12
  51.5 3.9 copy-start.4
  51.5 4.5 %copy-start.5 = (s32[2048]{0:T(1024)S(1)}, s32[2048]{0:T(1024)}, u32[]{:S(2)}) copy-start(s32[2048]{0:T(1024)} %param.14) | copy-start | bytes 24580
  55.4 54.7 %copy-start.10 = (s32[128]{0:T(128)}, s32[128]{0:T(128)S(1)}, u32[]{:S(2)}) copy-start(s32[128]{0:T(128)S(1)} %compare_select_fusion.3) | copy-start | bytes 1540
  113.7 38.0 %collective-permute-start = (bf16[128,400]{1,0:T(8,128)(2,1)S(1)}, bf16[128,400]{1,0:T(8,128)(2,1)}, u32[]{:S(2)}, u32[]{:S(2)}) collective-permute-start(bf16[128,400]{1,0:T(8,128)(2,1)S(1)} %gather_fusion.4), channel_id=1, source_target_pairs={{0,1},{1,2},{2,3},{3,4},{4,5},{5,6},{6,7},{7,0},{8,9},{9,10},{10,1... | collective-permute-start | bytes 307208 | tf_op jit(solution)/shard_map/ppermute | solution.py:30
  113.7 38.0 %collective-permute-start.1 = (bf16[128,400]{1,0:T(8,128)(2,1)S(1)}, bf16[128,400]{1,0:T(8,128)(2,1)S(1)}, u32[]{:S(2)}, u32[]{:S(2)}) collective-permute-start(bf16[128,400]{1,0:T(8,128)(2,1)S(1)} %gather_fusion.4), channel_id=1, source_target_pairs={{0,7},{1,0},{2,1},{3,2},{4,3},{5,4},{6,5},{7,6},{8,15},{9,8},{10,9... | collective-permute-start | bytes 307208 | tf_op jit(solution)/shard_map/ppermute | solution.py:33
  148.8 21.2 %copy-start = (bf16[2048,400]{0,1:T(8,128)(2,1)S(1)}, bf16[2048,400]{0,1:T(8,128)(2,1)}, u32[]{:S(2)}) copy-start(bf16[2048,400]{0,1:T(8,128)(2,1)} %copy.58) | copy-start | bytes 4915204
  151.7 6.6 %collective-permute-start.2 = (bf16[128,400]{1,0:T(8,128)(2,1)}, bf16[128,400]{1,0:T(8,128)(2,1)S(1)}, u32[]{:S(2)}, u32[]{:S(2)}) collective-permute-start(bf16[128,400]{1,0:T(8,128)(2,1)} %collective-permute-done), channel_id=1, source_target_pairs={{0,1},{1,2},{2,3},{3,4},{4,5},{5,6},{6,7},{7,0},{8,9},{9,10},{10,1... | collective-permute-start | bytes 307208 | tf_op jit(solution)/shard_map/ppermute | solution.py:30
  151.7 6.6 %collective-permute-start.3 = (bf16[128,400]{1,0:T(8,128)(2,1)S(1)}, bf16[128,400]{1,0:T(8,128)(2,1)S(1)}, u32[]{:S(2)}, u32[]{:S(2)}) collective-permute-start(bf16[128,400]{1,0:T(8,128)(2,1)S(1)} %collective-permute-done.1), channel_id=1, source_target_pairs={{0,7},{1,0},{2,1},{3,2},{4,3},{5,4},{6,5},{7,6},{8,15},{9,8},{10,9... | collective-permute-start | bytes 307208 | tf_op jit(solution)/shard_map/ppermute | solution.py:33
  158.3 6.4 %collective-permute-start.4 = (bf16[128,400]{1,0:T(8,128)(2,1)S(1)}, bf16[128,400]{1,0:T(8,128)(2,1)S(1)}, u32[]{:S(2)}, u32[]{:S(2)}) collective-permute-start(bf16[128,400]{1,0:T(8,128)(2,1)S(1)} %collective-permute-done.2), channel_id=1, source_target_pairs={{0,1},{1,2},{2,3},{3,4},{4,5},{5,6},{6,7},{7,0},{8,9},{9,10},{10,1... | collective-permute-start | bytes 307208 | tf_op jit(solution)/shard_map/ppermute | solution.py:30
  158.3 6.4 %collective-permute-start.5 = (bf16[128,400]{1,0:T(8,128)(2,1)S(1)}, bf16[128,400]{1,0:T(8,128)(2,1)S(1)}, u32[]{:S(2)}, u32[]{:S(2)}) collective-permute-start(bf16[128,400]{1,0:T(8,128)(2,1)S(1)} %collective-permute-done.3), channel_id=1, source_target_pairs={{0,7},{1,0},{2,1},{3,2},{4,3},{5,4},{6,5},{7,6},{8,15},{9,8},{10,9... | collective-permute-start | bytes 307208 | tf_op jit(solution)/shard_map/ppermute | solution.py:33
  164.7 5.3 %collective-permute-start.6 = (bf16[128,400]{1,0:T(8,128)(2,1)S(1)}, bf16[128,400]{1,0:T(8,128)(2,1)S(1)}, u32[]{:S(2)}, u32[]{:S(2)}) collective-permute-start(bf16[128,400]{1,0:T(8,128)(2,1)S(1)} %collective-permute-done.4), channel_id=1, source_target_pairs={{0,1},{1,2},{2,3},{3,4},{4,5},{5,6},{6,7},{7,0},{8,9},{9,10},{10,1... | collective-permute-start | bytes 307208 | tf_op jit(solution)/shard_map/ppermute | solution.py:30
  170.0 4.1 copy-start.3
  174.2 1.9 copy-start.1
  218.7 20.9 %copy-start.11 = (s32[128]{0:T(128)S(1)}, s32[128]{0:T(128)}, u32[]{:S(2)}) copy-start(s32[128]{0:T(128)} %copy-done.10) | copy-start | bytes 1540
  256.2 148.5 %copy-start.9 = (s32[32]{0:T(128)S(1)}, s32[32]{0:T(128)}, u32[]{:S(2)}) copy-start(s32[32]{0:T(128)} %copy-done.8) | copy-start | bytes 388
  404.8 4.5 %copy-start.7 = (f32[2048]{0:T(1024)S(1)}, f32[2048]{0:T(1024)}, u32[]{:S(2)}) copy-start(f32[2048]{0:T(1024)} %param.9) | copy-start | bytes 24580
  404.8 5.1 %copy-start.2 = (f32[2048,400]{0,1:T(8,128)S(1)}, f32[2048,400]{0,1:T(8,128)}, u32[]{:S(2)}) copy-start(f32[2048,400]{0,1:T(8,128)} %param.8) | copy-start | bytes 9830404
Sparse Core Ops, SparseCore 0:
  181.3 33.7 reduce-scatter.3
